TPU v7x, 32 devices: a whole 2x2x4 slice. The times are simulated.
32 devices in a mesh: groups: 2 (over y), space: 16 (over z, x, core).
Axes of the slice: x: 2, y: 2, z: 4, core: 2. Of those that a mesh axis runs over, the one named last changes fastest.
Arguments:
- modes: float32 [4, 128, 32, 64], P('groups', None, 'space'), parts along dimension 0, may hold values from -6 to 6
- cell_weight: float32 [32, 128], P('space', 'groups'), parts along dimension 1, may hold values from 0.5 to 2
- seeds: int32 [256], P(('groups', 'space')), parts along dimension 0, may hold values from 0 to 255
- coeff_table: float32 [256, 128], replicated, may hold values from -6 to 6
- force_table: float32 [256, 128], replicated, may hold values from -6 to 6
- visc_table: float32 [256], replicated, may hold values from 0.02 to 0.2
Outputs:
- coefficients: float32 [256, 128], P(('groups', 'space')), parts along dimension 0
There are 2 independent parts, one for each index of `groups`. A program takes and returns all parts, laid end to end along the dimension named above; an argument that names none is the same for every part. Nothing has to cross between parts.
All inputs are finite; a program needn't handle non-finite values.
Results may differ from a plain program's by a relative error of at most 0.00013.
Values sent between devices are 32-bit elements; how exact they have to be, the bound alone decides.
A program may use at most 64 MiB of HBM per device.

v0:
```python
import math
import jax
import jax.numpy as jnp
from jax import lax
from jax.sharding import PartitionSpec as P

STEPS = 2
TIME_STEP = 0.5


def padded_2(array, sides, width):
    for axis, dim in sides:
        devices, length = (lax.axis_size(axis), array.shape[dim])
        up = [(i, (i + 1) % devices) for i in range(devices)]
        down = [(j, i) for i, j in up]
        last = lax.slice_in_dim(array, length - width, length, axis=dim)
        first = lax.slice_in_dim(array, 0, width, axis=dim)
        before = lax.ppermute(last, axis, up)
        after = lax.ppermute(first, axis, down)
        array = jnp.concatenate([before, array, after], axis=dim)
    return array


def shards(modes, cell_weight, seeds, coeff_table, force_table, visc_table):
    mode_count = modes.shape[1]
    slab_cells = modes.shape[2]
    across = modes.shape[3]
    devices = lax.axis_size("space")
    cell_count = slab_cells * across
    total_cells = cell_count * devices
    padded = padded_2(modes, (("space", 2),), 2)
    slope_along = (
        padded[:, :, 0:slab_cells]
        - 8.0 * padded[:, :, 1 : slab_cells + 1]
        + 8.0 * padded[:, :, 3 : slab_cells + 3]
        - padded[:, :, 4 : slab_cells + 4]
    ) / 12.0
    slope_across = (
        jnp.roll(modes, 2, 3)
        - 8.0 * jnp.roll(modes, 1, 3)
        + 8.0 * jnp.roll(modes, -1, 3)
        - jnp.roll(modes, -2, 3)
    ) / 12.0
    slopes = jnp.stack([slope_along, slope_across]).reshape(2, 2, mode_count, cell_count)
    velocity = modes.reshape(2, mode_count, cell_count)
    cell_scale = cell_weight.reshape(cell_count) / total_cells
    weighted = velocity * cell_scale[None, None, :]
    diffusion = lax.psum(
        jnp.einsum(
            "taic,tajc->ij",
            slopes * cell_scale[None, None, None, :],
            slopes,
            precision=lax.Precision.HIGHEST,
        ),
        "space",
    )
    selector = (
        seeds[:, None] == jnp.arange(coeff_table.shape[0], dtype=jnp.int32)[None, :]
    ).astype(jnp.float32)
    coeffs = jnp.dot(selector, coeff_table, precision=lax.Precision.HIGHEST)
    forcing = jnp.dot(selector, force_table, precision=lax.Precision.HIGHEST)
    viscosity = jnp.dot(selector, visc_table, precision=lax.Precision.HIGHEST)
    own_count = coeffs.shape[0]

    def field_block(coeff_rows):
        flow = jnp.einsum("ni,aic->anc", coeff_rows, velocity, precision=lax.Precision.HIGHEST)
        grads = jnp.einsum("nk,takc->tanc", coeff_rows, slopes, precision=lax.Precision.HIGHEST)
        carried = jnp.sum(flow[:, None, :, :] * grads, axis=0)
        return jnp.einsum("aic,anc->ni", weighted, carried, precision=lax.Precision.HIGHEST)

    for repeat in range(STEPS):
        everyone = lax.all_gather(coeffs, "space", axis=0, tiled=True)
        rows_each = math.gcd(own_count * lax.axis_size("space"), 128)
        stacked = everyone.reshape(
            own_count * lax.axis_size("space") // rows_each, rows_each, mode_count
        )
        quadratic = lax.psum_scatter(
            lax.map(field_block, stacked).reshape(own_count * lax.axis_size("space"), mode_count),
            "space",
            scatter_dimension=0,
            tiled=True,
        )
        linear = jnp.dot(coeffs, diffusion, precision=lax.Precision.HIGHEST)
        coeffs = coeffs + TIME_STEP * (forcing - viscosity[:, None] * linear - quadratic)
    return coeffs


def solution(mesh):
    placed = (
        P("groups", None, "space", None),
        P("space", "groups"),
        P(("groups", "space")),
        P(),
        P(),
        P(),
    )
    return jax.shard_map(
        shards, mesh=mesh, in_specs=placed, out_specs=P(("groups", "space"), None), check_vma=False
    )
```

profile of v0, /device:TPU:8, one launch (start us, length us, event | category | flops | bytes accessed | tf_op | source)
XLA Modules:
  0.0 243.6 jit_solution(18027088971304564999)
XLA Ops:
  6.5 0.0 copy-start
  6.5 0.0 copy-start.1
  6.5 0.0 all-reduce.8.cloned.1.call-start
  6.5 0.0 collective-permute-start
  6.6 2.6 %collective-permute-start.1 = (f32[2,128,2,64]{1,3,2,0:T(8,128)}, f32[2,128,2,64]{1,3,2,0:T(8,128)S(1)}, u32[]{:S(2)}, u32[]{:S(2)}) collective-permute-start(f32[2,128,2,64]{1,3,2,0:T(8,128)} %param.6), channel_id=1, source_target_pairs={{1,0},{2,1},{3,2},{4,3},{5,4},{6,5},{7,6},{8,7},{9,8},{10,9},{11,1... | collective-permute-start | bytes 393224 | tf_op jit(solution)/shard_map/ppermute | solution.py:19
  9.2 1.0 slice_bitcast_fusion
  10.2 0.0 copy-done.1
  10.3 0.1 fusion.23
  10.3 0.0 copy-start.4
  10.3 0.1 copy.35
  10.4 0.0 copy-done
  10.4 0.5 copy-done.4
  11.0 0.2 fusion.34
  11.2 18.1 %all_gather.6 = f32[128,128]{1,0:T(8,128)S(1)} all-gather(f32[8,128]{1,0:T(8,128)S(1)} %fusion.34), channel_id=1, replica_groups=mesh['groups'=2,'space'=16] {'space'}, dimensions={0}, use_global_device_ids=true | all-gather | bytes 69632 | tf_op jit(solution)/shard_map/all_gather | solution.py:72
  29.2 0.1 copy.39
  29.3 0.3 convolution_bitcast_fusion.3
  29.6 0.0 copy-start.5
  29.6 0.0 copy-start.3
  29.6 0.1 copy.37
  29.8 0.6 copy-done.5
  30.3 0.1 div.18
  30.4 0.0 copy-start.7
  30.4 0.7 copy-done.7
  31.1 0.6 dynamic-slice.2
  32.3 0.0 copy-done.3
  32.3 0.2 fusion.33
  32.5 0.0 collective-permute-done
  32.5 0.0 collective-permute-done.1
  32.5 0.1 copy.34
  32.6 0.6 fusion.2
  33.2 1.0 convolution_bitcast_fusion.6
  34.3 1.0 convolution_bitcast_fusion.5
  35.3 0.0 all-reduce.8.cloned.1.call-update
  35.3 0.0 copy-start.6
  35.3 0.0 all-reduce.6.cloned.1.call-start
  35.4 0.6 copy-done.6
  36.0 0.2 convolution_bitcast_fusion.7
  36.2 90.3 %all-reduce.8.cloned.1.call-done = (f32[128,128]{1,0:T(8,128)}, f32[128,128]{1,0:T(8,128)}) async-done(((f32[128,128]{1,0:T(8,128)}, f32[128,128]{1,0:T(8,128)}), (f32[128,128]{1,0:T(8,128)}, f32[128,128]{1,0:T(8,128)})) %all-reduce.8.cloned.1.call-update) | async-done | bytes 131088 | tf_op jit(solution)/shard_map/psum | solution.py:48
  126.5 1.0 fusion.11
  127.4 16.9 %all_gather.7 = f32[128,128]{1,0:T(8,128)S(1)} all-gather(f32[8,128]{1,0:T(8,128)S(1)} %fusion.11), channel_id=1, replica_groups=mesh['groups'=2,'space'=16] {'space'}, dimensions={0}, use_global_device_ids=true | all-gather | bytes 69632 | tf_op jit(solution)/shard_map/all_gather | solution.py:72
  144.4 0.3 convolution_bitcast_fusion.2
  144.7 0.1 copy.42
  144.8 0.6 fusion.3
  145.4 1.0 convolution_bitcast_fusion.4
  146.4 0.0 all-reduce.6.cloned.1.call-update
  146.4 88.9 %all-reduce.6.cloned.1.call-done = f32[128,128]{1,0:T(8,128)} async-done(((f32[128,128]{1,0:T(8,128)}), f32[128,128]{1,0:T(8,128)}) %all-reduce.6.cloned.1.call-update) | async-done | bytes 65552
  235.3 0.0 copy-done.2
  235.3 1.4 fusion.7
  (6 shorter events, 0.1 us)
Async XLA Ops:
  6.5 3.9 %copy-start = (f32[256,128]{1,0:T(8,128)S(1)}, f32[256,128]{1,0:T(8,128)}, u32[]{:S(2)}) copy-start(f32[256,128]{1,0:T(8,128)} %param.9) | copy-start | bytes 393220
  6.5 3.6 %copy-start.1 = (f32[2,128,2,64]{1,3,2,0:T(8,128)S(1)}, f32[2,128,2,64]{1,3,2,0:T(8,128)}, u32[]{:S(2)}) copy-start(f32[2,128,2,64]{1,3,2,0:T(8,128)} %param.6) | copy-start | bytes 393220
  6.5 119.9 %all-reduce.8.cloned.1.call-start = ((), (), s32[]{:S(2)}) async-start(), calls=%async_computation.1 | async-start | bytes 262144 | tf_op jit(solution)/shard_map/psum | solution.py:48
  6.5 26.0 %collective-permute-start = (f32[2,128,2,64]{1,3,2,0:T(8,128)}, f32[2,128,2,64]{1,3,2,0:T(8,128)S(1)}, u32[]{:S(2)}, u32[]{:S(2)}) collective-permute-start(f32[2,128,2,64]{1,3,2,0:T(8,128)} %param.6), channel_id=1, source_target_pairs={{0,1},{1,2},{2,3},{3,4},{4,5},{5,6},{6,7},{7,8},{8,9},{9,10},{10,1... | collective-permute-start | bytes 393224 | tf_op jit(solution)/shard_map/ppermute | solution.py:18
  6.6 25.9 %collective-permute-start.1 = (f32[2,128,2,64]{1,3,2,0:T(8,128)}, f32[2,128,2,64]{1,3,2,0:T(8,128)S(1)}, u32[]{:S(2)}, u32[]{:S(2)}) collective-permute-start(f32[2,128,2,64]{1,3,2,0:T(8,128)} %param.6), channel_id=1, source_target_pairs={{1,0},{2,1},{3,2},{4,3},{5,4},{6,5},{7,6},{8,7},{9,8},{10,9},{11,1... | collective-permute-start | bytes 393224 | tf_op jit(solution)/shard_map/ppermute | solution.py:19
  10.3 0.7 copy-start.4
  29.6 0.7 copy-start.5
  29.6 2.7 %copy-start.3 = (f32[256,128]{1,0:T(8,128)S(1)}, f32[256,128]{1,0:T(8,128)}, u32[]{:S(2)}) copy-start(f32[256,128]{1,0:T(8,128)} %param.10) | copy-start | bytes 393220
  30.4 0.7 copy-start.7
  35.3 0.7 copy-start.6
  35.3 200.0 %all-reduce.6.cloned.1.call-start = ((), (), s32[]{:S(2)}) async-start(), calls=%async_computation | async-start | bytes 131072
  146.4 88.9 %copy-start.2 = (f32[128,128]{1,0:T(8,128)S(1)}, f32[128,128]{1,0:T(8,128)}, u32[]{:S(2)}) copy-start(f32[128,128]{1,0:T(8,128)} %get-tuple-element.27) | copy-start | bytes 196612
Sparse Core Ops, SparseCore 0:
  35.4 90.9 all-reduce.7
  146.5 88.7 all-reduce.5
where the time goes:
time: 244 us
  waiting for transfers between devices  179 us (73%)
  blocking collectives  35 us (14%)
  between operations  14.2 us (6%)
  matrix products  7.78 us (3%)
  local copies, waits for them, and re-layouts  4.56 us (2%)
  starting transfers between devices  2.68 us (1%)
    psum x1, waiting for transfers between devices, shards(): lax.psum(jnp.einsum('taic,tajc->ij', slopes * cell_scale[None, None, None...  90.3 us
    unnamed x3, waiting for transfers between devices  88.9 us
    all_gather x2, blocking collectives, shards(): everyone = lax.all_gather(coeffs, 'space', axis=0, tiled=True)  35 us
  transfers between devices with their start and end apart: 4, of which 2 were waited for; matrix products, arithmetic and copies ran while one was open for 1% of the time, Pallas kernels for 0%

commit v1 on v0

--- a/solution.py
+++ b/solution.py
@@ -6,6 +6,23 @@
 
 STEPS = 2
 TIME_STEP = 0.5
+
+
+def laid_out(blocks, dim):
+    blocks = jnp.moveaxis(blocks, 0, dim)
+    shape = blocks.shape
+    return blocks.reshape(*shape[:dim], shape[dim] * shape[dim + 1], *shape[dim + 2 :])
+
+
+def doubled(shard, axis):
+    size, mine = (lax.axis_size(axis), lax.axis_index(axis))
+    blocks, bit = (shard[None], 1)
+    while bit < size:
+        other = lax.ppermute(blocks, axis, [(i, i ^ bit) for i in range(size)])
+        low = mine & bit == 0
+        blocks = jnp.concatenate([jnp.where(low, blocks, other), jnp.where(low, other, blocks)])
+        bit *= 2
+    return blocks
 
 
 def padded_2(array, sides, width):
@@ -69,7 +86,7 @@
         return jnp.einsum("aic,anc->ni", weighted, carried, precision=lax.Precision.HIGHEST)
 
     for repeat in range(STEPS):
-        everyone = lax.all_gather(coeffs, "space", axis=0, tiled=True)
+        everyone = laid_out(doubled(coeffs, "space"), 0)
         rows_each = math.gcd(own_count * lax.axis_size("space"), 128)
         stacked = everyone.reshape(
             own_count * lax.axis_size("space") // rows_each, rows_each, mode_count

time: 244 us -> 234 us (0.959)
  blocking collectives: 35 us -> 0 us
  waiting for transfers between devices: 179 us -> 194 us
  starting transfers between devices: 2.68 us -> 12.8 us
    all_gather x2 -> x0, blocking collectives: 35 us -> none  [shards(): everyone = lax.all_gather(coeffs, 'space', axis=0, tiled=True)]
    ppermute x0 -> x8, waiting for transfers between devices: none -> 14.7 us  [doubled(): other = lax.ppermute(blocks, axis, [(i, i ^ bit) for i in range(size)])]
    ppermute x0 -> x8, starting transfers between devices: none -> 11.9 us  [doubled(): other = lax.ppermute(blocks, axis, [(i, i ^ bit) for i in range(size)])]
  transfers between devices with their start and end apart: 4 -> 12, of which waited for: 2 -> 8; matrix products, arithmetic and copies ran while one was open for 1% -> 1% of each run, Pallas kernels for 0% -> 0%
where the time goes in v1:
time: 234 us
  waiting for transfers between devices  194 us (83%)
  between operations  14.3 us (6%)
  starting transfers between devices  12.8 us (5%)
  matrix products  8.41 us (4%)
  local copies, waits for them, and re-layouts  3.41 us (1%)
    psum x1, waiting for transfers between devices, shards(): lax.psum(jnp.einsum('taic,tajc->ij', slopes * cell_scale[None, None, None...  91.9 us
    unnamed x3, waiting for transfers between devices  87.9 us
    ppermute x8, waiting for transfers between devices, doubled(): other = lax.ppermute(blocks, axis, [(i, i ^ bit) for i in range(size)])  14.7 us
    ppermute x8, starting transfers between devices, doubled(): other = lax.ppermute(blocks, axis, [(i, i ^ bit) for i in range(size)])  11.9 us
  transfers between devices with their start and end apart: 12, of which 8 were waited for; matrix products, arithmetic and copies ran while one was open for 1% of the time, Pallas kernels for 0%

profile of v1, /device:TPU:8, one launch (start us, length us, event | category | flops | bytes accessed | tf_op | source)
XLA Modules:
  0.0 233.6 jit_solution(4883397263140988671)
XLA Ops:
  6.5 0.8 collective-permute-start.1
  7.4 0.1 copy-done
  7.4 0.8 fusion.34
  8.3 0.8 collective-permute-start.2
  9.1 0.0 copy-start.3
  9.1 0.0 copy-start.4
  9.1 0.9 copy-done.3
  10.0 0.2 fusion.33
  10.2 2.4 %collective-permute-start.3 = (f32[2,8,128]{2,1,0:T(8,128)S(1)}, f32[2,8,128]{2,1,0:T(8,128)S(1)}, u32[]{:S(2)}, u32[]{:S(2)}) collective-permute-start(f32[2,8,128]{2,1,0:T(8,128)S(1)} %pad_maximum_fusion.13), channel_id=1, source_target_pairs={{0,2},{1,3},{2,0},{3,1},{4,6},{5,7},{6,4},{7,5},{8,10},{9,11},{10,... | collective-permute-start | bytes 24584 | tf_op jit(solution)/shard_map/ppermute | solution.py:21
  12.6 1.6 collective-permute-done.3
  14.3 2.5 %collective-permute-start.4 = (f32[4,8,128]{2,1,0:T(8,128)S(1)}, f32[4,8,128]{2,1,0:T(8,128)S(1)}, u32[]{:S(2)}, u32[]{:S(2)}) collective-permute-start(f32[4,8,128]{2,1,0:T(8,128)S(1)} %pad_maximum_fusion.11), channel_id=1, source_target_pairs={{0,4},{1,5},{2,6},{3,7},{4,0},{5,1},{6,2},{7,3},{8,12},{9,13},{10,... | collective-permute-start | bytes 49160 | tf_op jit(solution)/shard_map/ppermute | solution.py:21
  16.8 1.7 collective-permute-done.4
  18.5 4.0 %collective-permute-start.5 = (f32[8,8,128]{2,1,0:T(8,128)S(1)}, f32[8,8,128]{2,1,0:T(8,128)S(1)}, u32[]{:S(2)}, u32[]{:S(2)}) collective-permute-start(f32[8,8,128]{2,1,0:T(8,128)S(1)} %pad_maximum_fusion.9), channel_id=1, source_target_pairs={{0,8},{1,9},{2,10},{3,11},{4,12},{5,13},{6,14},{7,15},{8,0},{9,1},... | collective-permute-start | bytes 98312 | tf_op jit(solution)/shard_map/ppermute | solution.py:21
  22.5 0.1 fusion.23
  22.6 0.1 div.18
  22.7 0.1 copy.35
  22.8 0.1 copy.39
  22.9 0.0 copy-start.7
  22.9 0.6 copy-done.7
  23.6 0.6 dynamic-slice
  24.8 0.3 convolution_bitcast_fusion.3
  25.1 0.1 copy.37
  25.3 0.1 copy.34
  25.4 1.0 convolution_bitcast_fusion.6
  26.4 0.6 fusion.2
  27.0 1.0 convolution_bitcast_fusion.5
  28.0 0.0 all-reduce.8.cloned.1.call-update
  28.0 0.0 copy-start.6
  28.0 0.0 all-reduce.6.cloned.1.call-start
  28.1 0.6 copy-done.6
  28.7 0.2 convolution_bitcast_fusion.7
  28.9 91.9 %all-reduce.8.cloned.1.call-done = (f32[128,128]{1,0:T(8,128)}, f32[128,128]{1,0:T(8,128)}) async-done(((f32[128,128]{1,0:T(8,128)}, f32[128,128]{1,0:T(8,128)}), (f32[128,128]{1,0:T(8,128)}, f32[128,128]{1,0:T(8,128)})) %all-reduce.8.cloned.1.call-update) | async-done | bytes 131088 | tf_op jit(solution)/shard_map/psum | solution.py:65
  120.8 1.0 fusion.11
  121.8 0.1 collective-permute-start.6
  121.8 1.2 collective-permute-done.6
  123.0 0.6 collective-permute-start.7
  123.6 3.1 %collective-permute-done.7 = f32[2,8,128]{2,1,0:T(8,128)S(1)} collective-permute-done((f32[2,8,128]{2,1,0:T(8,128)S(1)}, f32[2,8,128]{2,1,0:T(8,128)S(1)}, u32[]{:S(2)}, u32[]{:S(2)}) %collective-permute-start.7) | collective-permute-done | bytes 8224 | tf_op jit(solution)/shard_map/ppermute | solution.py:21
  126.7 0.1 collective-permute-start.8
  126.7 3.7 %collective-permute-done.8 = f32[4,8,128]{2,1,0:T(8,128)S(1)} collective-permute-done((f32[4,8,128]{2,1,0:T(8,128)S(1)}, f32[4,8,128]{2,1,0:T(8,128)S(1)}, u32[]{:S(2)}, u32[]{:S(2)}) %collective-permute-start.8) | collective-permute-done | bytes 16416 | tf_op jit(solution)/shard_map/ppermute | solution.py:21
  130.5 1.5 collective-permute-start.9
  132.0 3.4 %collective-permute-done.9 = f32[8,8,128]{2,1,0:T(8,128)S(1)} collective-permute-done((f32[8,8,128]{2,1,0:T(8,128)S(1)}, f32[8,8,128]{2,1,0:T(8,128)S(1)}, u32[]{:S(2)}, u32[]{:S(2)}) %collective-permute-start.9) | collective-permute-done | bytes 32800 | tf_op jit(solution)/shard_map/ppermute | solution.py:21
  135.4 0.3 convolution_bitcast_fusion.2
  135.6 0.1 copy.42
  135.7 0.6 fusion.3
  136.3 1.0 convolution_bitcast_fusion.4
  137.4 0.0 all-reduce.6.cloned.1.call-update
  137.4 87.9 %all-reduce.6.cloned.1.call-done = f32[128,128]{1,0:T(8,128)} async-done(((f32[128,128]{1,0:T(8,128)}), f32[128,128]{1,0:T(8,128)}) %all-reduce.6.cloned.1.call-update) | async-done | bytes 65552
  225.3 1.5 fusion.7
  (34 shorter events, 0.2 us)
Async XLA Ops:
  6.5 0.9 copy-start
  6.5 2.5 %copy-start.1 = (f32[2,128,2,64]{1,3,2,0:T(8,128)S(1)}, f32[2,128,2,64]{1,3,2,0:T(8,128)}, u32[]{:S(2)}) copy-start(f32[2,128,2,64]{1,3,2,0:T(8,128)} %param.6) | copy-start | bytes 393220
  6.5 114.2 %all-reduce.8.cloned.1.call-start = ((), (), s32[]{:S(2)}) async-start(), calls=%async_computation.1 | async-start | bytes 262144 | tf_op jit(solution)/shard_map/psum | solution.py:65
  6.5 18.7 %collective-permute-start.1 = (f32[2,128,2,64]{1,3,2,0:T(8,128)}, f32[2,128,2,64]{1,3,2,0:T(8,128)S(1)}, u32[]{:S(2)}, u32[]{:S(2)}) collective-permute-start(f32[2,128,2,64]{1,3,2,0:T(8,128)} %param.6), channel_id=1, source_target_pairs={{1,0},{2,1},{3,2},{4,3},{5,4},{6,5},{7,6},{8,7},{9,8},{10,9},{11,1... | collective-permute-start | bytes 393224 | tf_op jit(solution)/shard_map/ppermute | solution.py:36
  7.4 17.9 %collective-permute-start = (f32[2,128,2,64]{1,3,2,0:T(8,128)}, f32[2,128,2,64]{1,3,2,0:T(8,128)S(1)}, u32[]{:S(2)}, u32[]{:S(2)}) collective-permute-start(f32[2,128,2,64]{1,3,2,0:T(8,128)} %param.6), channel_id=1, source_target_pairs={{0,1},{1,2},{2,3},{3,4},{4,5},{5,6},{6,7},{7,8},{8,9},{9,10},{10,1... | collective-permute-start | bytes 393224 | tf_op jit(solution)/shard_map/ppermute | solution.py:35
  8.3 1.9 collective-permute-start.2
  9.1 0.9 copy-start.3
  9.1 0.9 copy-start.4
  10.2 4.0 %collective-permute-start.3 = (f32[2,8,128]{2,1,0:T(8,128)S(1)}, f32[2,8,128]{2,1,0:T(8,128)S(1)}, u32[]{:S(2)}, u32[]{:S(2)}) collective-permute-start(f32[2,8,128]{2,1,0:T(8,128)S(1)} %pad_maximum_fusion.13), channel_id=1, source_target_pairs={{0,2},{1,3},{2,0},{3,1},{4,6},{5,7},{6,4},{7,5},{8,10},{9,11},{10,... | collective-permute-start | bytes 24584 | tf_op jit(solution)/shard_map/ppermute | solution.py:21
  14.2 2.6 %copy-start.5 = (f32[2,64]{1,0:T(2,128)S(1)}, f32[2,64]{1,0:T(2,128)}, u32[]{:S(2)}) copy-start(f32[2,64]{1,0:T(2,128)} %param.7) | copy-start | bytes 1540
  14.3 4.3 %collective-permute-start.4 = (f32[4,8,128]{2,1,0:T(8,128)S(1)}, f32[4,8,128]{2,1,0:T(8,128)S(1)}, u32[]{:S(2)}, u32[]{:S(2)}) collective-permute-start(f32[4,8,128]{2,1,0:T(8,128)S(1)} %pad_maximum_fusion.11), channel_id=1, source_target_pairs={{0,4},{1,5},{2,6},{3,7},{4,0},{5,1},{6,2},{7,3},{8,12},{9,13},{10,... | collective-permute-start | bytes 49160 | tf_op jit(solution)/shard_map/ppermute | solution.py:21
  18.5 6.3 %collective-permute-start.5 = (f32[8,8,128]{2,1,0:T(8,128)S(1)}, f32[8,8,128]{2,1,0:T(8,128)S(1)}, u32[]{:S(2)}, u32[]{:S(2)}) collective-permute-start(f32[8,8,128]{2,1,0:T(8,128)S(1)} %pad_maximum_fusion.9), channel_id=1, source_target_pairs={{0,8},{1,9},{2,10},{3,11},{4,12},{5,13},{6,14},{7,15},{8,0},{9,1},... | collective-permute-start | bytes 98312 | tf_op jit(solution)/shard_map/ppermute | solution.py:21
  22.9 0.7 copy-start.7
  28.0 0.7 copy-start.6
  28.0 197.3 %all-reduce.6.cloned.1.call-start = ((), (), s32[]{:S(2)}) async-start(), calls=%async_computation | async-start | bytes 131072
  121.8 1.2 collective-permute-start.6
  123.0 3.7 %collective-permute-start.7 = (f32[2,8,128]{2,1,0:T(8,128)S(1)}, f32[2,8,128]{2,1,0:T(8,128)S(1)}, u32[]{:S(2)}, u32[]{:S(2)}) collective-permute-start(f32[2,8,128]{2,1,0:T(8,128)S(1)} %pad_maximum_fusion.14), channel_id=1, source_target_pairs={{0,2},{1,3},{2,0},{3,1},{4,6},{5,7},{6,4},{7,5},{8,10},{9,11},{10,... | collective-permute-start | bytes 24584 | tf_op jit(solution)/shard_map/ppermute | solution.py:21
  126.7 3.8 %collective-permute-start.8 = (f32[4,8,128]{2,1,0:T(8,128)S(1)}, f32[4,8,128]{2,1,0:T(8,128)S(1)}, u32[]{:S(2)}, u32[]{:S(2)}) collective-permute-start(f32[4,8,128]{2,1,0:T(8,128)S(1)} %pad_maximum_fusion.12), channel_id=1, source_target_pairs={{0,4},{1,5},{2,6},{3,7},{4,0},{5,1},{6,2},{7,3},{8,12},{9,13},{10,... | collective-permute-start | bytes 49160 | tf_op jit(solution)/shard_map/ppermute | solution.py:21
  130.5 4.9 %collective-permute-start.9 = (f32[8,8,128]{2,1,0:T(8,128)S(1)}, f32[8,8,128]{2,1,0:T(8,128)S(1)}, u32[]{:S(2)}, u32[]{:S(2)}) collective-permute-start(f32[8,8,128]{2,1,0:T(8,128)S(1)} %pad_maximum_fusion.10), channel_id=1, source_target_pairs={{0,8},{1,9},{2,10},{3,11},{4,12},{5,13},{6,14},{7,15},{8,0},{9,1},... | collective-permute-start | bytes 98312 | tf_op jit(solution)/shard_map/ppermute | solution.py:21
  137.4 87.9 %copy-start.2 = (f32[128,128]{1,0:T(8,128)S(1)}, f32[128,128]{1,0:T(8,128)}, u32[]{:S(2)}) copy-start(f32[128,128]{1,0:T(8,128)} %get-tuple-element.27) | copy-start | bytes 196612
Sparse Core Ops, SparseCore 0:
  28.1 92.6 all-reduce.7
  137.5 87.7 all-reduce.5
